TPU v7x, 32 devices: a whole 2x2x4 slice. The times are simulated.
32 devices in a mesh: run: 8 (over z, core), mz: 4 (over y, x).
Axes of the slice: x: 2, y: 2, z: 4, core: 2. Of those that a mesh axis runs over, the one named last changes fastest.
Arguments:
- lcms: bfloat16 [512, 256, 4096], P('run', None, 'mz'), may hold values from -600 to 600
- spectra: float32 [512, 65536], P('run', 'mz'), may hold values from -200 to 200
- scan_factor: float32 [64, 256], replicated, may hold values from 0.05 to 0.9
- mz_factor: float32 [64, 4096], P(None, 'mz'), may hold values from 0 to 1.7
- ppm_factor: float32 [64, 65536], P(None, 'mz'), may hold values from 0 to 1.7
Outputs:
- sample_factor: float32 [512, 64], P('run')
- ppm_new: float32 [64, 65536], P(None, ('mz', 'run'))
All inputs are finite; a program needn't handle non-finite values.
Results may differ from a plain program's by a relative error of at most 0.0048.
Values sent between devices are 32-bit elements; how exact they have to be, the bound alone decides.
No kernel may reach another device: no remote copies, remote signals or barrier semaphores. Data moves between devices by JAX's collectives and lax.ppermute only.
A program may use at most 128 MiB of HBM per device.

v0:
```python
import jax
import jax.numpy as jnp
from jax import lax
from jax.sharding import PartitionSpec as P


def solve_rows(gram_matrix, right_rows):
    lower_factor = jnp.linalg.cholesky(gram_matrix)
    return jax.scipy.linalg.cho_solve((lower_factor, True), right_rows.T).T


def per_device(lcms, spectra, scan_factor, mz_factor, ppm_factor):
    highest = lax.Precision.HIGHEST
    shared_spectra = lax.all_to_all(spectra, "run", split_axis=1, concat_axis=0, tiled=True)
    scan_bf = scan_factor.astype(jnp.bfloat16)
    tensor = jnp.einsum("ijk,rj->irk", lcms, scan_bf, preferred_element_type=jnp.float32)
    lcms_local = jnp.sum(tensor * mz_factor[None], axis=2)
    nmr_local = lax.dot_general(spectra, ppm_factor, (((1,), (1,)), ((), ())), precision=highest)
    mz_local = jnp.dot(mz_factor, mz_factor.T, precision=highest)
    ppm_local = jnp.dot(ppm_factor, ppm_factor.T, precision=highest)
    mz_gram, ppm_gram = lax.psum((mz_local, ppm_local), "mz")
    lcms_part, nmr_part = lax.psum((lcms_local, nmr_local), "mz")
    lcms_gram = jnp.dot(scan_factor, scan_factor.T, precision=highest) * mz_gram
    sample_first = solve_rows(lcms_gram + ppm_gram, lcms_part + nmr_part)
    whole_rows = lax.all_gather(sample_first, "run", axis=0, tiled=True)
    sample_gram = lax.psum(jnp.dot(sample_first.T, sample_first, precision=highest), "run")
    projected = jnp.dot(whole_rows.T, shared_spectra, precision=highest)
    ppm_new = jax.scipy.linalg.cho_solve((jnp.linalg.cholesky(sample_gram), True), projected)
    gram_local = jnp.dot(ppm_new, ppm_new.T, precision=highest)
    new_gram = lax.psum(gram_local, ("run", "mz"))
    fit_local = lax.dot_general(
        shared_spectra, ppm_new, (((1,), (1,)), ((), ())), precision=highest
    )
    fit_owned = lax.psum_scatter(fit_local, "run", scatter_dimension=0, tiled=True)
    nmr_fit = lax.psum(fit_owned, "mz")
    sample_factor = solve_rows(lcms_gram + new_gram, lcms_part + nmr_fit)
    return (sample_factor, ppm_new)


def solution(mesh):
    return jax.shard_map(
        per_device,
        mesh=mesh,
        in_specs=(P("run", None, "mz"), P("run", "mz"), P(), P(None, "mz"), P(None, "mz")),
        out_specs=(P("run", None), P(None, ("mz", "run"))),
        check_vma=False,
    )
```

profile of v0, /device:TPU:0, one launch (start us, length us, event | category | flops | bytes accessed | tf_op | source)
XLA Modules:
  0.0 250.2 jit_solution(10968291417373203832)
XLA Ops:
  7.2 4.7 %copy.56 = f32[8,8,8,2048]{3,2,0,1:T(8,128)} copy(f32[8,8,8,2048]{3,2,1,0:T(8,128)} %bitcast.76) | data formatting | bytes 8388608 | tf_op jit(solution)/shard_map/all_to_all | solution.py:14
  11.8 6.5 %all-to-all-start = ((f32[64,8,2048]{2,0,1:T(8,128)}), f32[64,8,2048]{2,0,1:T(8,128)}, u32[]{:S(2)}, u32[]{:S(2)}) async-start(f32[64,8,2048]{2,0,1:T(8,128)} %bitcast.77), calls=%async_computation | async-start | bytes 8388608 | tf_op jit(solution)/shard_map/all_to_all | solution.py:14
  18.3 0.0 all-reduce.3.cloned.1.call-start
  18.4 0.0 copy-done.2
  18.4 1.0 fusion.28
  19.3 7.7 %fusion.30 = f32[64,64]{1,0:T(8,128)} fusion(f32[64,16384]{1,0:T(8,128)} %param.9, f32[64,16384]{1,0:T(8,128)} %param.12), kind=kOutput, calls=%fused_computation.47 | convolution fusion | flops 805306368 | bytes 8404992 | tf_op jit(solution)/shard_map/dot_general | solution.py:18
  27.0 0.0 copy-done
  27.0 4.0 %fusion.29 = f32[64,64]{0,1:T(8,128)} fusion(f32[64,16384]{1,0:T(8,128)S(1)} %copy-done), kind=kOutput, calls=%fused_computation.46 | convolution fusion | flops 805306368 | bytes 4210688 | tf_op jit(solution)/shard_map/dot_general | solution.py:20
  31.0 17.2 %multiply_reduce_fusion = f32[64,64]{0,1:T(8,128)} fusion(bf16[64,256,1024]{2,1,0:T(8,128)(2,1)} %param.8, f32[64,1024]{1,0:T(8,128)S(1)} %copy-done.2, f32[64,256]{1,0:T(8,128)S(1)} %copy-done.3), kind=kOutput, calls=%fused_computation | convolution fusion | flops 2155884544 | bytes 33898496 | tf_op jit(solution)/shard_map/ijk,rj->irk/dot_general | solution.py:16
  48.2 0.0 all-reduce.3.cloned.1.call-update
  48.2 0.2 reduce-scatter.2.cloned.1.call-start
  48.4 44.0 %all-reduce.3.cloned.1.call-done = (f32[64,64]{0,1:T(8,128)}, f32[64,64]{0,1:T(8,128)}, f32[64,64]{1,0:T(8,128)}, f32[64,64]{1,0:T(8,128)}) async-done(((f32[64,64]{0,1:T(8,128)}, f32[64,64]{0,1:T(8,128)}, f32[64,64]{1,0:T(8,128)}, f32[64,64]{1,0:T(8,128)}), (f32[64,64]{0,1:T(8,128)}, f32[64,64]{0,1:T(8,128)}, f32[64,64]{1,0:T(8,128)}, f32[64,64]{1,0:T(8,128)})) %all-reduce.3.cloned.1.call-update) | async-done | bytes 65552 | tf_op jit(solution)/shard_map/psum | solution.py:21
  92.4 1.0 fusion.27
  93.4 0.1 copy.39
  93.5 5.8 %cholesky.59 = f32[64,64]{1,0:T(8,128)S(1)} custom-call(f32[64,64]{1,0:T(8,128)S(1)} %fusion.19), custom_call_target="Cholesky" | custom-call | tf_op jit(solution)/shard_map/jit(cholesky)/cholesky | solution.py:8
  99.4 0.6 compare_reduce_fusion.2
  100.0 0.7 fusion
  100.7 4.9 %custom-call.16 = f32[1,64,64]{1,2,0:T(8,128)S(1)} custom-call(f32[1,64,64]{2,1,0:T(8,128)S(1)} %fusion), custom_call_target="InvertDiagBlocksLowerTriangular" | custom-call | tf_op jit(solution)/shard_map/jit(_cho_solve)/triangular_solve | solution.py:9
  105.6 1.0 fusion.13
  106.6 0.2 fusion.16
  106.8 0.1 copy.42
  106.9 0.2 fusion.31
  107.1 28.0 %psum.53 = f32[64,64]{0,1:T(8,128)S(1)} all-reduce(f32[64,64]{0,1:T(8,128)S(1)} %fusion.31), channel_id=1, replica_groups=mesh['run'=8,'mz'=4] {'run'}, use_global_device_ids=true, to_apply=%region_7.10 | all-reduce | flops 4096 | bytes 32768 | tf_op jit(solution)/shard_map/psum | solution.py:26
  135.1 0.1 copy.41
  135.2 5.8 %cholesky.70 = f32[64,64]{1,0:T(8,128)S(1)} custom-call(f32[64,64]{1,0:T(8,128)S(1)} %fusion.12), custom_call_target="Cholesky" | custom-call | tf_op jit(solution)/shard_map/jit(cholesky)/cholesky | solution.py:28
  141.1 0.6 compare_reduce_fusion.1
  141.7 0.7 fusion.1
  142.4 4.9 %custom-call.14 = f32[1,64,64]{1,2,0:T(8,128)S(1)} custom-call(f32[1,64,64]{2,1,0:T(8,128)S(1)} %fusion.1), custom_call_target="InvertDiagBlocksLowerTriangular" | custom-call | tf_op jit(solution)/shard_map/jit(_cho_solve)/triangular_solve | solution.py:28
  147.3 14.2 %all_gather.3 = f32[512,64]{1,0:T(8,128)S(1)} all-gather(f32[64,64]{1,0:T(8,128)S(1)} %copy.42), channel_id=1, replica_groups=mesh['run'=8,'mz'=4] {'run'}, dimensions={0}, use_global_device_ids=true | all-gather | bytes 147456 | tf_op jit(solution)/shard_map/all_gather | solution.py:25
  161.5 0.0 all-to-all-done
  161.5 4.8 %fusion.32 = f32[64,2048]{1,0:T(8,128)S(1)} fusion(f32[512,64]{1,0:T(8,128)S(1)} %all_gather.3, f32[512,2048]{1,0:T(8,128)} %bitcast.11), kind=kOutput, calls=%fused_computation.49 | convolution fusion | flops 805306368 | bytes 4849664 | tf_op jit(solution)/shard_map/dot_general | solution.py:27
  166.3 0.6 fusion.10
  166.9 0.6 fusion.8
  167.5 0.0 copy-start.1
  167.5 6.5 %convolution_bitcast_fusion = f32[512,64]{1,0:T(8,128)} fusion(f32[64,2048]{1,0:T(8,128)S(1)} %fusion.8, f32[512,2048]{1,0:T(8,128)} %bitcast.11), kind=kOutput, calls=%fused_computation.2 | convolution fusion | flops 805306368 | bytes 4849664 | tf_op jit(solution)/shard_map/dot_general | solution.py:31
  174.0 0.6 fusion.33
  174.6 0.0 reduce-scatter.2.cloned.1.call-update
  174.6 37.8 %psum.54 = f32[64,64]{0,1:T(8,128)S(1)} all-reduce(f32[64,64]{0,1:T(8,128)S(1)} %fusion.33), channel_id=1, replica_groups=mesh['run'=8,'mz'=4] {'run','mz'}, use_global_device_ids=true, to_apply=%region_8.11 | all-reduce | flops 4096 | bytes 32768 | tf_op jit(solution)/shard_map/psum | solution.py:30
  212.4 0.1 copy.45
  212.5 5.8 %cholesky.81 = f32[64,64]{1,0:T(8,128)S(1)} custom-call(f32[64,64]{1,0:T(8,128)S(1)} %fusion.7), custom_call_target="Cholesky" | custom-call | tf_op jit(solution)/shard_map/jit(cholesky)/cholesky | solution.py:8
  218.4 0.6 compare_reduce_fusion
  219.0 0.7 fusion.2
  219.7 4.9 %custom-call.17 = f32[1,64,64]{1,2,0:T(8,128)S(1)} custom-call(f32[1,64,64]{2,1,0:T(8,128)S(1)} %fusion.2), custom_call_target="InvertDiagBlocksLowerTriangular" | custom-call | tf_op jit(solution)/shard_map/jit(_cho_solve)/triangular_solve | solution.py:9
  224.6 0.0 reduce-scatter.2.cloned.1.call-done
  224.6 17.7 %psum.55 = f32[64,64]{1,0:T(8,128)S(1)} all-reduce(f32[64,64]{1,0:T(8,128)} %reduce-scatter.2.cloned.1.call-done), channel_id=1, replica_groups=mesh['run'=8,'mz'=4] {'mz'}, use_global_device_ids=true, to_apply=%region_10.13 | all-reduce | flops 4096 | bytes 32768 | tf_op jit(solution)/shard_map/psum | solution.py:35
  242.3 0.2 fusion.3
  242.5 0.2 convolution_bitcast_fusion.1
  242.7 0.7 copy.47
  (14 shorter events, 0.1 us)
Async XLA Ops:
  11.8 6.5 %copy-start.2 = (f32[64,1024]{1,0:T(8,128)S(1)}, f32[64,1024]{1,0:T(8,128)}, u32[]{:S(2)}) copy-start(f32[64,1024]{1,0:T(8,128)} %param.11) | copy-start | bytes 786436
  11.8 149.6 %all-to-all-start = ((f32[64,8,2048]{2,0,1:T(8,128)}), f32[64,8,2048]{2,0,1:T(8,128)}, u32[]{:S(2)}, u32[]{:S(2)}) async-start(f32[64,8,2048]{2,0,1:T(8,128)} %bitcast.77), calls=%async_computation | async-start | bytes 8388608 | tf_op jit(solution)/shard_map/all_to_all | solution.py:14
  18.3 74.1 %all-reduce.3.cloned.1.call-start = ((), (), s32[]{:S(2)}) async-start(), calls=%async_computation.3 | async-start | bytes 262144 | tf_op jit(solution)/shard_map/psum | solution.py:21
  19.3 7.7 %copy-start = (f32[64,16384]{1,0:T(8,128)S(1)}, f32[64,16384]{1,0:T(8,128)}, u32[]{:S(2)}) copy-start(f32[64,16384]{1,0:T(8,128)} %param.12) | copy-start | bytes 12582916
  27.0 4.0 %copy-start.3 = (f32[64,256]{1,0:T(8,128)S(1)}, f32[64,256]{1,0:T(8,128)}, u32[]{:S(2)}) copy-start(f32[64,256]{1,0:T(8,128)} %param.10) | copy-start | bytes 196612
  48.2 176.4 %reduce-scatter.2.cloned.1.call-start = ((), (), s32[]{:S(2)}) async-start(), calls=%async_computation.2 | async-start | bytes 294912 | tf_op jit(solution)/shard_map/reduce_scatter | solution.py:34
  166.9 75.4 %copy-start.4 = (f32[64,64]{1,0:T(8,128)S(1)}, f32[64,64]{1,0:T(8,128)}, u32[]{:S(2)}) copy-start(f32[64,64]{1,0:T(8,128)} %get-tuple-element.14) | copy-start | bytes 49156
  167.5 75.9 %copy-start.1 = (f32[64,2048]{1,0:T(8,128)}, f32[64,2048]{1,0:T(8,128)S(1)}, u32[]{:S(2)}) copy-start(f32[64,2048]{1,0:T(8,128)S(1)} %fusion.8) | copy-start | bytes 1572868
Sparse Core Ops, SparseCore 0:
  48.3 44.0 all-reduce.2
  174.7 28.0 reduce-scatter.1
where the time goes:
time: 251 us; the launch traced here: 250 us
  blocking collectives  97.7 us (39%)
  matrix products  45.6 us (18%)
  waiting for transfers between devices  44.1 us (18%)
  other arithmetic  36.2 us (14%)
  between operations  14.2 us (6%)
  starting transfers between devices  6.74 us (3%)
  local copies, waits for them, and re-layouts  5.68 us (2%)
    psum x1, waiting for transfers between devices, per_device(): mz_gram, ppm_gram = lax.psum((mz_local, ppm_local), 'mz')  44 us
    psum x1, blocking collectives, per_device(): new_gram = lax.psum(gram_local, ('run', 'mz'))  37.8 us
    psum x1, blocking collectives, per_device(): lax.psum(jnp.dot(sample_first.T, sample_first, precision=highest), 'run')  28 us
    psum x1, blocking collectives, per_device(): nmr_fit = lax.psum(fit_owned, 'mz')  17.7 us
    dot_general x1, matrix products, per_device(): jnp.einsum('ijk,rj->irk', lcms, scan_bf, preferred_element_type=jnp.float32)  17.2 us
    all_gather x1, blocking collectives, per_device(): whole_rows = lax.all_gather(sample_first, 'run', axis=0, tiled=True)  14.2 us
    another operation x6, other arithmetic, solve_rows(): lower_factor = jnp.linalg.cholesky(gram_matrix)  13 us
    another operation x4, other arithmetic, solve_rows(): return jax.scipy.linalg.cho_solve((lower_factor, True), right_rows.T).T  11.1 us
  transfers between devices with their start and end apart: 3, of which 1 were waited for; matrix products, arithmetic and copies ran while one was open for 27% of the time, Pallas kernels for 0%

commit v1 on v0

--- a/solution.py
+++ b/solution.py
@@ -27,7 +27,7 @@
     projected = jnp.dot(whole_rows.T, shared_spectra, precision=highest)
     ppm_new = jax.scipy.linalg.cho_solve((jnp.linalg.cholesky(sample_gram), True), projected)
     gram_local = jnp.dot(ppm_new, ppm_new.T, precision=highest)
-    new_gram = lax.psum(gram_local, ("run", "mz"))
+    new_gram = lax.psum(lax.psum(gram_local, "mz"), "run")
     fit_local = lax.dot_general(
         shared_spectra, ppm_new, (((1,), (1,)), ((), ())), precision=highest
     )

time: 251 us -> 266 us (1.060)
  waiting for transfers between devices: 44.1 us -> 71.6 us
  blocking collectives: 97.7 us -> 85.6 us
    reduce_scatter x1, waiting for transfers between devices: 0.03 us -> 27.6 us  [per_device(): lax.psum_scatter(fit_local, 'run', scatter_dimension=0, tiled=True)]
    psum x2, blocking collectives: 55.5 us -> 43.4 us  [per_device(): new_gram = lax.psum(lax.psum(gram_local, 'mz'), 'run')]
  transfers between devices with their start and end apart: 3 -> 3, of which waited for: 1 -> 2; matrix products, arithmetic and copies ran while one was open for 27% -> 21% of each run, Pallas kernels for 0% -> 0%
where the time goes in v1:
time: 266 us
  blocking collectives  85.6 us (32%)
  waiting for transfers between devices  71.6 us (27%)
  matrix products  45.6 us (17%)
  other arithmetic  36.2 us (14%)
  between operations  14.2 us (5%)
  starting transfers between devices  6.74 us (3%)
  local copies, waits for them, and re-layouts  5.69 us (2%)
    psum x1, waiting for transfers between devices, per_device(): mz_gram, ppm_gram = lax.psum((mz_local, ppm_local), 'mz')  44 us
    psum x2, blocking collectives, per_device(): new_gram = lax.psum(lax.psum(gram_local, 'mz'), 'run')  43.4 us
    psum x1, blocking collectives, per_device(): lax.psum(jnp.dot(sample_first.T, sample_first, precision=highest), 'run')  28 us
    reduce_scatter x1, waiting for transfers between devices, per_device(): lax.psum_scatter(fit_local, 'run', scatter_dimension=0, tiled=True)  27.6 us
    dot_general x1, matrix products, per_device(): jnp.einsum('ijk,rj->irk', lcms, scan_bf, preferred_element_type=jnp.float32)  17.2 us
    all_gather x1, blocking collectives, per_device(): whole_rows = lax.all_gather(sample_first, 'run', axis=0, tiled=True)  14.2 us
    another operation x6, other arithmetic, solve_rows(): lower_factor = jnp.linalg.cholesky(gram_matrix)  13 us
    another operation x4, other arithmetic, solve_rows(): return jax.scipy.linalg.cho_solve((lower_factor, True), right_rows.T).T  11.1 us
  transfers between devices with their start and end apart: 3, of which 2 were waited for; matrix products, arithmetic and copies ran while one was open for 21% of the time, Pallas kernels for 0%

profile of v1, /device:TPU:0, one launch (start us, length us, event | category | flops | bytes accessed | tf_op | source)
XLA Modules:
  0.0 265.7 jit_solution(4890407910668177663)
XLA Ops:
  7.2 4.7 %copy.56 = f32[8,8,8,2048]{3,2,0,1:T(8,128)} copy(f32[8,8,8,2048]{3,2,1,0:T(8,128)} %bitcast.76) | data formatting | bytes 8388608 | tf_op jit(solution)/shard_map/all_to_all | solution.py:14
  11.8 6.5 %all-to-all-start = ((f32[64,8,2048]{2,0,1:T(8,128)}), f32[64,8,2048]{2,0,1:T(8,128)}, u32[]{:S(2)}, u32[]{:S(2)}) async-start(f32[64,8,2048]{2,0,1:T(8,128)} %bitcast.77), calls=%async_computation | async-start | bytes 8388608 | tf_op jit(solution)/shard_map/all_to_all | solution.py:14
  18.3 0.0 all-reduce.4.cloned.1.call-start
  18.4 0.0 copy-done.2
  18.4 1.0 fusion.28
  19.3 7.7 %fusion.30 = f32[64,64]{1,0:T(8,128)} fusion(f32[64,16384]{1,0:T(8,128)} %param.9, f32[64,16384]{1,0:T(8,128)} %param.12), kind=kOutput, calls=%fused_computation.47 | convolution fusion | flops 805306368 | bytes 8404992 | tf_op jit(solution)/shard_map/dot_general | solution.py:18
  27.0 4.0 %fusion.29 = f32[64,64]{0,1:T(8,128)} fusion(f32[64,16384]{1,0:T(8,128)S(1)} %copy-done), kind=kOutput, calls=%fused_computation.46 | convolution fusion | flops 805306368 | bytes 4210688 | tf_op jit(solution)/shard_map/dot_general | solution.py:20
  31.0 17.2 %multiply_reduce_fusion = f32[64,64]{0,1:T(8,128)} fusion(bf16[64,256,1024]{2,1,0:T(8,128)(2,1)} %param.8, f32[64,1024]{1,0:T(8,128)S(1)} %copy-done.2, f32[64,256]{1,0:T(8,128)S(1)} %copy-done.3), kind=kOutput, calls=%fused_computation | convolution fusion | flops 2155884544 | bytes 33898496 | tf_op jit(solution)/shard_map/ijk,rj->irk/dot_general | solution.py:16
  48.2 0.0 all-reduce.4.cloned.1.call-update
  48.2 0.2 reduce-scatter.2.cloned.1.call-start
  48.4 44.0 %all-reduce.4.cloned.1.call-done = (f32[64,64]{0,1:T(8,128)}, f32[64,64]{0,1:T(8,128)}, f32[64,64]{1,0:T(8,128)}, f32[64,64]{1,0:T(8,128)}) async-done(((f32[64,64]{0,1:T(8,128)}, f32[64,64]{0,1:T(8,128)}, f32[64,64]{1,0:T(8,128)}, f32[64,64]{1,0:T(8,128)}), (f32[64,64]{0,1:T(8,128)}, f32[64,64]{0,1:T(8,128)}, f32[64,64]{1,0:T(8,128)}, f32[64,64]{1,0:T(8,128)})) %all-reduce.4.cloned.1.call-update) | async-done | bytes 65552 | tf_op jit(solution)/shard_map/psum | solution.py:21
  92.4 1.0 fusion.27
  93.4 0.1 copy.39
  93.5 5.8 %cholesky.59 = f32[64,64]{1,0:T(8,128)S(1)} custom-call(f32[64,64]{1,0:T(8,128)S(1)} %fusion.19), custom_call_target="Cholesky" | custom-call | tf_op jit(solution)/shard_map/jit(cholesky)/cholesky | solution.py:8
  99.4 0.6 compare_reduce_fusion.2
  100.0 0.7 fusion
  100.7 4.9 %custom-call.16 = f32[1,64,64]{1,2,0:T(8,128)S(1)} custom-call(f32[1,64,64]{2,1,0:T(8,128)S(1)} %fusion), custom_call_target="InvertDiagBlocksLowerTriangular" | custom-call | tf_op jit(solution)/shard_map/jit(_cho_solve)/triangular_solve | solution.py:9
  105.6 1.0 fusion.13
  106.6 0.2 fusion.16
  106.8 0.1 copy.42
  106.9 0.2 fusion.31
  107.1 28.0 %psum.60 = f32[64,64]{0,1:T(8,128)S(1)} all-reduce(f32[64,64]{0,1:T(8,128)S(1)} %fusion.31), channel_id=1, replica_groups=mesh['run'=8,'mz'=4] {'run'}, use_global_device_ids=true, to_apply=%region_7.10 | all-reduce | flops 4096 | bytes 32768 | tf_op jit(solution)/shard_map/psum | solution.py:26
  135.1 0.1 copy.41
  135.2 5.8 %cholesky.70 = f32[64,64]{1,0:T(8,128)S(1)} custom-call(f32[64,64]{1,0:T(8,128)S(1)} %fusion.12), custom_call_target="Cholesky" | custom-call | tf_op jit(solution)/shard_map/jit(cholesky)/cholesky | solution.py:28
  141.1 0.6 compare_reduce_fusion.1
  141.7 0.7 fusion.1
  142.4 4.9 %custom-call.14 = f32[1,64,64]{1,2,0:T(8,128)S(1)} custom-call(f32[1,64,64]{2,1,0:T(8,128)S(1)} %fusion.1), custom_call_target="InvertDiagBlocksLowerTriangular" | custom-call | tf_op jit(solution)/shard_map/jit(_cho_solve)/triangular_solve | solution.py:28
  147.3 14.2 %all_gather.3 = f32[512,64]{1,0:T(8,128)S(1)} all-gather(f32[64,64]{1,0:T(8,128)S(1)} %copy.42), channel_id=1, replica_groups=mesh['run'=8,'mz'=4] {'run'}, dimensions={0}, use_global_device_ids=true | all-gather | bytes 147456 | tf_op jit(solution)/shard_map/all_gather | solution.py:25
  161.5 0.0 all-to-all-done
  161.5 4.8 %fusion.32 = f32[64,2048]{1,0:T(8,128)S(1)} fusion(f32[512,64]{1,0:T(8,128)S(1)} %all_gather.3, f32[512,2048]{1,0:T(8,128)} %bitcast.11), kind=kOutput, calls=%fused_computation.49 | convolution fusion | flops 805306368 | bytes 4849664 | tf_op jit(solution)/shard_map/dot_general | solution.py:27
  166.3 0.6 fusion.10
  166.9 0.6 fusion.8
  167.5 0.0 copy-start.1
  167.5 6.5 %convolution_bitcast_fusion = f32[512,64]{1,0:T(8,128)} fusion(f32[64,2048]{1,0:T(8,128)S(1)} %fusion.8, f32[512,2048]{1,0:T(8,128)} %bitcast.11), kind=kOutput, calls=%fused_computation.2 | convolution fusion | flops 805306368 | bytes 4849664 | tf_op jit(solution)/shard_map/dot_general | solution.py:31
  174.0 0.0 reduce-scatter.2.cloned.1.call-update
  174.0 0.6 fusion.33
  174.6 27.6 %reduce-scatter.2.cloned.1.call-done = f32[64,64]{1,0:T(8,128)} async-done(((f32[512,64]{1,0:T(8,128)}), f32[64,64]{1,0:T(8,128)}) %reduce-scatter.2.cloned.1.call-update) | async-done | bytes 16400 | tf_op jit(solution)/shard_map/reduce_scatter | solution.py:34
  202.2 17.4 %all-reduce = (f32[64,64]{0,1:T(8,128)S(1)}, f32[64,64]{1,0:T(8,128)S(1)}) all-reduce(f32[64,64]{0,1:T(8,128)S(1)} %fusion.33, f32[64,64]{1,0:T(8,128)} %reduce-scatter.2.cloned.1.call-done), channel_id=1, replica_groups=mesh['run'=8,'mz'=4] {'mz'}, use_global_device_ids=true, to_apply=%region_8.11 | all-reduce | flops 8192 | bytes 65536 | tf_op jit(solution)/shard_map/psum | solution.py:30
  219.6 25.9 %psum.62 = f32[64,64]{0,1:T(8,128)S(1)} all-reduce(f32[64,64]{0,1:T(8,128)S(1)} %get-tuple-element.12), channel_id=1, replica_groups=mesh['run'=8,'mz'=4] {'run'}, use_global_device_ids=true, to_apply=%region_9.12 | all-reduce | flops 4096 | bytes 32768 | tf_op jit(solution)/shard_map/psum | solution.py:30
  245.6 0.1 copy.45
  245.7 5.8 %cholesky.81 = f32[64,64]{1,0:T(8,128)S(1)} custom-call(f32[64,64]{1,0:T(8,128)S(1)} %fusion.7), custom_call_target="Cholesky" | custom-call | tf_op jit(solution)/shard_map/jit(cholesky)/cholesky | solution.py:8
  251.6 0.6 compare_reduce_fusion
  252.2 0.7 fusion.2
  252.9 4.9 %custom-call.17 = f32[1,64,64]{1,2,0:T(8,128)S(1)} custom-call(f32[1,64,64]{2,1,0:T(8,128)S(1)} %fusion.2), custom_call_target="InvertDiagBlocksLowerTriangular" | custom-call | tf_op jit(solution)/shard_map/jit(_cho_solve)/triangular_solve | solution.py:9
  257.8 0.0 copy-done.4
  257.8 0.2 fusion.3
  258.0 0.2 convolution_bitcast_fusion.1
  258.2 0.7 copy.47
  (14 shorter events, 0.1 us)
Async XLA Ops:
  11.8 6.5 %copy-start.2 = (f32[64,1024]{1,0:T(8,128)S(1)}, f32[64,1024]{1,0:T(8,128)}, u32[]{:S(2)}) copy-start(f32[64,1024]{1,0:T(8,128)} %param.11) | copy-start | bytes 786436
  11.8 149.6 %all-to-all-start = ((f32[64,8,2048]{2,0,1:T(8,128)}), f32[64,8,2048]{2,0,1:T(8,128)}, u32[]{:S(2)}, u32[]{:S(2)}) async-start(f32[64,8,2048]{2,0,1:T(8,128)} %bitcast.77), calls=%async_computation | async-start | bytes 8388608 | tf_op jit(solution)/shard_map/all_to_all | solution.py:14
  18.3 74.1 %all-reduce.4.cloned.1.call-start = ((), (), s32[]{:S(2)}) async-start(), calls=%async_computation.3 | async-start | bytes 262144 | tf_op jit(solution)/shard_map/psum | solution.py:21
  19.3 7.7 %copy-start = (f32[64,16384]{1,0:T(8,128)S(1)}, f32[64,16384]{1,0:T(8,128)}, u32[]{:S(2)}) copy-start(f32[64,16384]{1,0:T(8,128)} %param.12) | copy-start | bytes 12582916
  27.0 4.0 %copy-start.3 = (f32[64,256]{1,0:T(8,128)S(1)}, f32[64,256]{1,0:T(8,128)}, u32[]{:S(2)}) copy-start(f32[64,256]{1,0:T(8,128)} %param.10) | copy-start | bytes 196612
  48.2 154.0 %reduce-scatter.2.cloned.1.call-start = ((), (), s32[]{:S(2)}) async-start(), calls=%async_computation.2 | async-start | bytes 294912 | tf_op jit(solution)/shard_map/reduce_scatter | solution.py:34
  166.9 90.9 %copy-start.4 = (f32[64,64]{1,0:T(8,128)S(1)}, f32[64,64]{1,0:T(8,128)}, u32[]{:S(2)}) copy-start(f32[64,64]{1,0:T(8,128)} %get-tuple-element.16) | copy-start | bytes 49156
  167.5 91.4 %copy-start.1 = (f32[64,2048]{1,0:T(8,128)}, f32[64,2048]{1,0:T(8,128)S(1)}, u32[]{:S(2)}) copy-start(f32[64,2048]{1,0:T(8,128)S(1)} %fusion.8) | copy-start | bytes 1572868
Sparse Core Ops, SparseCore 0:
  48.3 44.0 all-reduce.3
  174.1 28.0 reduce-scatter.1
